TPU v7x, 128 devices: a whole 4x4x4 slice. The times are simulated.
128 devices in a mesh: row: 8 (over y, z_lo), col: 16 (over x, z_hi, core).
Axes of the slice: x: 4, y: 4, z: 4 (z_hi: 2, z_lo: 2; z = z_hi * 2 + z_lo), core: 2. Of those that a mesh axis runs over, the one named last changes fastest.
Arguments:
- tokens: bfloat16 [4096, 6144], P('row', 'col'), may hold values from -40 to 40
- ln_gain: float32 [6144], replicated, may hold values from 0.25 to 1.75
- w_qkv: bfloat16 [6144, 3, 4096], P('row', None, 'col'), may hold values from -0.078125 to 0.078125
- q_gain: float32 [128], replicated, may hold values from 0.1 to 1.9
- k_gain: float32 [128], replicated, may hold values from 0.1 to 1.9
- w_up: bfloat16 [6144, 12288], P('row', 'col'), may hold values from -0.078125 to 0.078125
- w_out: bfloat16 [4096, 6144], P('col', 'row'), may hold values from -0.5 to 0.5
- w_down: bfloat16 [12288, 6144], P('col', 'row'), may hold values from -0.078125 to 0.078125
Outputs:
- mixed: bfloat16 [4096, 6144], P('row', 'col')
All inputs are finite; a program needn't handle non-finite values.
Results may differ from a plain program's by a relative error of at most 0.017.
Values may be sent and summed in bfloat16 or wider, within the bound.
No kernel may reach another device: no remote copies, remote signals or barrier semaphores. Data moves between devices by JAX's collectives and lax.ppermute only.
A program may use at most 128 MiB of HBM per device.

v0:
```python
import math
import jax
import jax.numpy as jnp
from jax import lax
from jax.sharding import PartitionSpec as P

HD = 128
PATCHES = 256
epsilon = 1e-06


def layer_norm(values_in, gain_vec):
    x_float = values_in.astype(jnp.float32)
    centre = jnp.mean(x_float, axis=-1, keepdims=True)
    deviation = x_float - centre
    variance = jnp.mean(deviation * deviation, axis=-1, keepdims=True)
    return deviation * lax.rsqrt(variance + epsilon) * gain_vec


def attend(projected, q_gain, k_gain):
    tok_count = projected.shape[0]
    frame_count = tok_count // PATCHES
    arranged = projected.reshape(frame_count, PATCHES, 3, -1, HD)
    queries = layer_norm(arranged[:, :, 0], q_gain).astype(jnp.bfloat16)
    key_vecs = layer_norm(arranged[:, :, 1], k_gain).astype(jnp.bfloat16)
    value_vecs = arranged[:, :, 2].astype(jnp.bfloat16)
    scores = jnp.einsum(
        "fqhd,fkhd->fhqk", queries, key_vecs, preferred_element_type=jnp.float32
    ) / math.sqrt(HD)
    exponent = jnp.exp(scores)
    attn_probs = (exponent / jnp.sum(exponent, axis=-1, keepdims=True)).astype(jnp.bfloat16)
    attended = jnp.einsum(
        "fhqk,fkhd->fqhd", attn_probs, value_vecs, preferred_element_type=jnp.float32
    )
    return attended.astype(jnp.bfloat16).reshape(tok_count, -1)


def shards(tokens, ln_gain, w_qkv, q_gain, k_gain, w_up, w_out, w_down):
    gathered = lax.all_gather(tokens, "col", axis=1, tiled=True)
    normed = layer_norm(gathered, ln_gain).astype(jnp.bfloat16)

    def add_rows(weight_rows):
        flattened = weight_rows.reshape(weight_rows.shape[0], -1)
        return jnp.dot(normed, flattened, preferred_element_type=jnp.float32)

    weight_rows = (
        lax.all_gather(w_qkv, "row", axis=0, tiled=True),
        lax.all_gather(w_up, "row", axis=0, tiled=True),
    )
    projected = add_rows(weight_rows[0])
    pre_act = add_rows(weight_rows[1])
    attended = attend(projected, q_gain, k_gain)
    activated = jax.nn.gelu(pre_act, approximate=False).astype(jnp.bfloat16)
    column_block = jnp.dot(
        attended,
        lax.all_gather(w_out, "row", axis=1, tiled=True),
        preferred_element_type=jnp.float32,
    )
    column_block = column_block + jnp.dot(
        activated,
        lax.all_gather(w_down, "row", axis=1, tiled=True),
        preferred_element_type=jnp.float32,
    )
    summed = lax.psum_scatter(
        column_block.astype(jnp.bfloat16), "col", scatter_dimension=1, tiled=True
    ).astype(jnp.float32)
    return (tokens.astype(jnp.float32) + summed).astype(jnp.bfloat16)


def solution(mesh):
    in_specs = (
        P("row", "col"),
        P(),
        P("row", None, "col"),
        P(),
        P(),
        P("row", "col"),
        P("col", "row"),
        P("col", "row"),
    )
    out_specs = P("row", "col")
    return jax.shard_map(shards, mesh=mesh, in_specs=in_specs, out_specs=out_specs, check_vma=False)
```

profile of v0, /device:TPU:0, one launch (start us, length us, event | category | flops | bytes accessed | tf_op | source)
XLA Modules:
  0.0 848.3 jit_solution(13845213418589235404)
XLA Ops:
  6.5 0.7 all-gather.6.cloned.1.call-update
  7.3 2.4 copy.17
  9.8 0.7 all-gather.14.cloned.1.call-update
  10.5 0.5 all-gather.12.cloned.1.call-update
  11.1 0.5 all-gather.10.cloned.1.call-update
  11.7 70.0 %all-gather.6.cloned.1.call-done = bf16[512,6144]{1,0:T(8,128)(2,1)} async-done(((bf16[512,384]{1,0:T(8,128)(2,1)}), bf16[512,6144]{1,0:T(8,128)(2,1)}) %all-gather.6.cloned.1.call-update) | async-done | bytes 6291472 | tf_op jit(solution)/shard_map/all_gather | solution.py:39
  81.6 3.8 convert_reduce_fusion
  85.5 0.7 copy-done
  86.2 1.8 fusion.2
  88.0 6.3 fusion.4
  94.3 175.4 %all-gather.8.cloned.1.call-done = bf16[6144,3,256]{0,2,1:T(8,128)(2,1)} async-done(((bf16[768,3,256]{0,2,1:T(8,128)(2,1)}), bf16[6144,3,256]{0,2,1:T(8,128)(2,1)}) %all-gather.8.cloned.1.call-update) | async-done | bytes 9437200 | tf_op jit(solution)/shard_map/all_gather | solution.py:47
  269.8 9.5 %fusion.93 = f32[2,256,3,2,128]{1,4,3,2,0:T(8,128)S(1)} fusion(bf16[2,256,6144,1,1]{2,1,4,3,0:T(8,128)(2,1)} %bitcast.46, bf16[3,2,128,6144,1]{3,2,1,0,4:T(8,128)(2,1)} %bitcast.49), kind=kOutput, calls=%fused_computation.121 | convolution fusion | flops 4831838208 | bytes 17301504 | tf_op jit(solution)/shard_map/dot_general | solution.py:44
  279.6 0.4 copy-done.3
  280.0 0.4 fusion.15
  280.4 0.3 fusion.16
  280.9 181.7 %all-gather.14.cloned.1.call-done = bf16[768,6144]{1,0:T(8,128)(2,1)} async-done(((bf16[768,768]{1,0:T(8,128)(2,1)}), bf16[768,6144]{1,0:T(8,128)(2,1)}) %all-gather.14.cloned.1.call-update) | async-done | bytes 9437200 | tf_op jit(solution)/shard_map/all_gather | solution.py:61
  462.6 192.6 %all-gather.12.cloned.1.call-done = bf16[6144,768]{1,0:T(8,128)(2,1)} async-done(((bf16[768,768]{1,0:T(8,128)(2,1)}), bf16[6144,768]{1,0:T(8,128)(2,1)}) %all-gather.12.cloned.1.call-update) | async-done | bytes 9437200 | tf_op jit(solution)/shard_map/all_gather | solution.py:48
  655.2 26.3 %fusion.17 = f32[512,6144]{1,0:T(8,128)} fusion(bf16[768,6144]{1,0:T(8,128)(2,1)} %all-gather.14.cloned.1.call-done, bf16[512,6144]{1,0:T(8,128)(2,1)} %fusion.4, bf16[6144,768]{1,0:T(8,128)(2,1)} %all-gather.12.cloned.1.call-done), kind=kOutput, calls=%fused_computation.32 | convolution fusion | flops 9689235456 | bytes 37748736 | tf_op jit(solution)/shard_map/dot_general | solution.py:59
  681.5 48.4 %all-gather.10.cloned.1.call-done = bf16[256,6144]{1,0:T(8,128)(2,1)} async-done(((bf16[256,768]{1,0:T(8,128)(2,1)}), bf16[256,6144]{1,0:T(8,128)(2,1)}) %all-gather.10.cloned.1.call-update) | async-done | bytes 3145744 | tf_op jit(solution)/shard_map/all_gather | solution.py:56
  729.9 9.9 %add_convert_fusion = bf16[512,6144]{1,0:T(8,128)(2,1)} fusion(f32[512,6144]{1,0:T(8,128)} %fusion.17, bf16[256,6144]{1,0:T(8,128)(2,1)} %all-gather.10.cloned.1.call-done, bf16[64,8,2,128]{3,2,1,0:T(2,128)(2,1)S(1)} %bitcast.47), kind=kOutput, calls=%fused_computation.7 | convolution fusion | flops 1616904192 | bytes 22282240 | tf_op jit(solution)/shard_map/dot_general | solution.py:54
  739.8 8.7 %copy.26 = bf16[512,6144]{0,1:T(8,128)(2,1)} copy(bf16[512,6144]{1,0:T(8,128)(2,1)} %add_convert_fusion) | data formatting | bytes 12582912
  748.5 90.9 %reduce-scatter.4.cloned.1.call-done = bf16[384,512]{1,0:T(8,128)(2,1)} async-done(((bf16[6144,512]{1,0:T(8,128)(2,1)}), bf16[384,512]{1,0:T(8,128)(2,1)}) %reduce-scatter.4.cloned.1.call-update) | async-done | bytes 393232
  839.4 1.2 copy.27
  840.7 0.8 add_convert_fusion.1
  (24 shorter events, 0.7 us)
Async XLA Ops:
  6.5 75.1 %all-gather.6.cloned.1.call-start = ((), (), s32[]{:S(2)}) async-start(), calls=%async_computation.1 | async-start | bytes 6684672 | tf_op jit(solution)/shard_map/all_gather | solution.py:39
  7.3 262.5 %all-gather.8.cloned.1.call-start = ((), (), s32[]{:S(2)}) async-start(), calls=%async_computation.2 | async-start | bytes 10616832 | tf_op jit(solution)/shard_map/all_gather | solution.py:47
  9.7 452.8 %all-gather.14.cloned.1.call-start = ((), (), s32[]{:S(2)}) async-start(), calls=%async_computation.5 | async-start | bytes 10616832 | tf_op jit(solution)/shard_map/all_gather | solution.py:61
  10.5 644.7 %all-gather.12.cloned.1.call-start = ((), (), s32[]{:S(2)}) async-start(), calls=%async_computation.4 | async-start | bytes 10616832 | tf_op jit(solution)/shard_map/all_gather | solution.py:48
  11.0 718.9 %all-gather.10.cloned.1.call-start = ((), (), s32[]{:S(2)}) async-start(), calls=%async_computation.3 | async-start | bytes 3538944 | tf_op jit(solution)/shard_map/all_gather | solution.py:56
  11.6 827.8 %reduce-scatter.4.cloned.1.call-start = ((), (), s32[]{:S(2)}) async-start(), calls=%async_computation.6 | async-start | bytes 6684672
  81.6 4.6 copy-start
  86.2 1.8 copy-start.2
  279.3 0.7 copy-start.3
  279.3 0.7 copy-start.4
  748.5 92.1 %copy-start.1 = (bf16[512,384]{1,0:T(8,128)(2,1)S(1)}, bf16[512,384]{1,0:T(8,128)(2,1)}, u32[]{:S(2)}) copy-start(bf16[512,384]{1,0:T(8,128)(2,1)} %param.8) | copy-start | bytes 1179652
Sparse Core Ops, SparseCore 0:
  9.6 71.9 all-gather.5
  83.3 186.4 all-gather.7
  271.4 191.0 all-gather.13
  464.1 191.0 all-gather.11
  656.7 73.1 all-gather.9
  748.7 90.7 reduce-scatter.3
where the time goes:
time: 849 us; the launch traced here: 848 us
  waiting for transfers between devices  761 us (90%)
  matrix products  46.5 us (5%)
  local copies, waits for them, and re-layouts  13.6 us (2%)
  between operations  13.6 us (2%)
  other arithmetic  13 us (2%)
    all_gather x1, waiting for transfers between devices, shards(): lax.all_gather(w_up, 'row', axis=0, tiled=True)  193 us
    all_gather x1, waiting for transfers between devices, shards(): lax.all_gather(w_down, 'row', axis=1, tiled=True)  182 us
    all_gather x1, waiting for transfers between devices, shards(): lax.all_gather(w_qkv, 'row', axis=0, tiled=True)  175 us
    unnamed x7, waiting for transfers between devices  93.4 us
    all_gather x1, waiting for transfers between devices, shards(): gathered = lax.all_gather(tokens, 'col', axis=1, tiled=True)  70 us
    all_gather x1, waiting for transfers between devices, shards(): lax.all_gather(w_out, 'row', axis=1, tiled=True)  48.4 us
    dot_general x1, matrix products, shards(): jnp.dot(activated, lax.all_gather(w_down, 'row', axis=1, tiled=True), pre...  26.3 us
  transfers between devices with their start and end apart: 6, of which 6 were waited for; matrix products, arithmetic and copies ran while one was open for 6% of the time, Pallas kernels for 0%

commit v1 on v0

--- a/solution.py
+++ b/solution.py
@@ -58,7 +58,9 @@
     )
     column_block = column_block + jnp.dot(
         activated,
-        lax.all_gather(w_down, "row", axis=1, tiled=True),
+        jnp.concatenate(
+            lax.all_to_all(jnp.stack([w_down] * lax.axis_size("row")), "row", 0, 0), axis=1
+        ),
         preferred_element_type=jnp.float32,
     )
     summed = lax.psum_scatter(

time: 849 us -> 738 us (0.87)
  waiting for transfers between devices: 761 us -> 640 us
    all_gather x1 -> x0, waiting for transfers between devices: 182 us -> none  [shards(): lax.all_gather(w_down, 'row', axis=1, tiled=True)]
    all_gather x1, waiting for transfers between devices: 70 us -> 142 us  [shards(): gathered = lax.all_gather(tokens, 'col', axis=1, tiled=True)]
    all_gather x1, waiting for transfers between devices: 193 us -> 182 us  [shards(): lax.all_gather(w_up, 'row', axis=0, tiled=True)]
    unnamed x7 -> x6, waiting for transfers between devices: 93.4 us -> 92.8 us
  transfers between devices with their start and end apart: 6 -> 6, of which waited for: 6 -> 5; matrix products, arithmetic and copies ran while one was open for 6% -> 8% of each run, Pallas kernels for 0% -> 0%
where the time goes in v1:
time: 738 us
  waiting for transfers between devices  640 us (87%)
  matrix products  46.5 us (6%)
  local copies, waits for them, and re-layouts  18.9 us (3%)
  between operations  13.2 us (2%)
  other arithmetic  13 us (2%)
    all_gather x1, waiting for transfers between devices, shards(): lax.all_gather(w_up, 'row', axis=0, tiled=True)  182 us
    all_gather x1, waiting for transfers between devices, shards(): lax.all_gather(w_qkv, 'row', axis=0, tiled=True)  175 us
    all_gather x1, waiting for transfers between devices, shards(): gathered = lax.all_gather(tokens, 'col', axis=1, tiled=True)  142 us
    unnamed x6, waiting for transfers between devices  92.8 us
    all_gather x1, waiting for transfers between devices, shards(): lax.all_gather(w_out, 'row', axis=1, tiled=True)  48.5 us
    dot_general x1, matrix products, shards(): jnp.dot(activated, jnp.concatenate(lax.all_to_all(jnp.stack([w_down] * la...  26.2 us
  transfers between devices with their start and end apart: 6, of which 5 were waited for; matrix products, arithmetic and copies ran while one was open for 8% of the time, Pallas kernels for 0%

profile of v1, /device:TPU:0, one launch (start us, length us, event | category | flops | bytes accessed | tf_op | source)
XLA Modules:
  0.0 737.9 jit_solution(1862557681402801996)
XLA Ops:
  6.5 0.7 all-gather.5.cloned.1.call-update
  7.3 2.4 copy.18
  9.8 0.7 all-gather.11.cloned.1.call-update
  10.5 0.5 copy-done.2
  11.0 0.6 copy.23
  11.6 4.1 stack.2
  15.7 5.9 all-to-all-start
  21.7 0.5 all-gather.9.cloned.1.call-update
  22.3 142.0 %all-gather.5.cloned.1.call-done = bf16[512,6144]{1,0:T(8,128)(2,1)} async-done(((bf16[512,384]{1,0:T(8,128)(2,1)}), bf16[512,6144]{1,0:T(8,128)(2,1)}) %all-gather.5.cloned.1.call-update) | async-done | bytes 6291472 | tf_op jit(solution)/shard_map/all_gather | solution.py:39
  164.3 3.8 convert_reduce_fusion
  168.1 0.7 copy-done
  168.9 1.8 fusion.2
  170.7 6.3 fusion.4
  177.0 175.2 %all-gather.7.cloned.1.call-done = bf16[6144,3,256]{0,2,1:T(8,128)(2,1)} async-done(((bf16[768,3,256]{0,2,1:T(8,128)(2,1)}), bf16[6144,3,256]{0,2,1:T(8,128)(2,1)}) %all-gather.7.cloned.1.call-update) | async-done | bytes 9437200 | tf_op jit(solution)/shard_map/all_gather | solution.py:47
  352.1 9.5 %fusion.93 = f32[2,256,3,2,128]{1,4,3,2,0:T(8,128)S(1)} fusion(bf16[2,256,6144,1,1]{2,1,4,3,0:T(8,128)(2,1)} %bitcast.49, bf16[3,2,128,6144,1]{3,2,1,0,4:T(8,128)(2,1)} %bitcast.52), kind=kOutput, calls=%fused_computation.121 | convolution fusion | flops 4831838208 | bytes 17301504 | tf_op jit(solution)/shard_map/dot_general | solution.py:44
  362.3 0.4 fusion.15
  363.3 181.6 %all-gather.11.cloned.1.call-done = bf16[6144,768]{1,0:T(8,128)(2,1)} async-done(((bf16[768,768]{1,0:T(8,128)(2,1)}), bf16[6144,768]{1,0:T(8,128)(2,1)}) %all-gather.11.cloned.1.call-update) | async-done | bytes 9437200 | tf_op jit(solution)/shard_map/all_gather | solution.py:48
  544.9 26.2 %fusion.17 = f32[512,6144]{1,0:T(8,128)} fusion(bf16[768,6144]{0,1:T(8,128)(2,1)} %bitcast.12, bf16[512,6144]{1,0:T(8,128)(2,1)} %fusion.4, bf16[6144,768]{1,0:T(8,128)(2,1)} %all-gather.11.cloned.1.call-done), kind=kOutput, calls=%fused_computation.32 | convolution fusion | flops 9689235456 | bytes 37748736 | tf_op jit(solution)/shard_map/dot_general | solution.py:59
  571.2 48.5 %all-gather.9.cloned.1.call-done = bf16[256,6144]{1,0:T(8,128)(2,1)} async-done(((bf16[256,768]{1,0:T(8,128)(2,1)}), bf16[256,6144]{1,0:T(8,128)(2,1)}) %all-gather.9.cloned.1.call-update) | async-done | bytes 3145744 | tf_op jit(solution)/shard_map/all_gather | solution.py:56
  619.6 10.0 %add_convert_fusion = bf16[512,6144]{1,0:T(8,128)(2,1)} fusion(f32[512,6144]{1,0:T(8,128)} %fusion.17, bf16[256,6144]{1,0:T(8,128)(2,1)} %all-gather.9.cloned.1.call-done, bf16[64,8,2,128]{3,2,1,0:T(2,128)(2,1)S(1)} %bitcast.50), kind=kOutput, calls=%fused_computation.7 | convolution fusion | flops 1616904192 | bytes 22282240 | tf_op jit(solution)/shard_map/dot_general | solution.py:54
  629.7 8.7 %copy.28 = bf16[512,6144]{0,1:T(8,128)(2,1)} copy(bf16[512,6144]{1,0:T(8,128)(2,1)} %add_convert_fusion) | data formatting | bytes 12582912
  638.4 90.9 %reduce-scatter.4.cloned.1.call-done = bf16[384,512]{1,0:T(8,128)(2,1)} async-done(((bf16[6144,512]{1,0:T(8,128)(2,1)}), bf16[384,512]{1,0:T(8,128)(2,1)}) %reduce-scatter.4.cloned.1.call-update) | async-done | bytes 393232
  729.3 1.2 copy.29
  730.5 0.8 add_convert_fusion.1
  (27 shorter events, 1.3 us)
Async XLA Ops:
  6.5 157.7 %all-gather.5.cloned.1.call-start = ((), (), s32[]{:S(2)}) async-start(), calls=%async_computation.2 | async-start | bytes 6684672 | tf_op jit(solution)/shard_map/all_gather | solution.py:39
  7.3 344.9 %all-gather.7.cloned.1.call-start = ((), (), s32[]{:S(2)}) async-start(), calls=%async_computation.3 | async-start | bytes 10616832 | tf_op jit(solution)/shard_map/all_gather | solution.py:47
  9.7 1.3 copy-start.2
  9.7 535.2 %all-gather.11.cloned.1.call-start = ((), (), s32[]{:S(2)}) async-start(), calls=%async_computation.5 | async-start | bytes 10616832 | tf_op jit(solution)/shard_map/all_gather | solution.py:48
  15.7 347.6 %all-to-all-start = ((bf16[8,768,768]{1,2,0:T(8,128)(2,1)}), bf16[8,768,768]{1,2,0:T(8,128)(2,1)}, u32[]{:S(2)}, u32[]{:S(2)}) async-start(bf16[8,768,768]{1,2,0:T(8,128)(2,1)} %stack.2), calls=%async_computation | async-start | bytes 18874368 | tf_op jit(solution)/shard_map/all_to_all | solution.py:62
  21.6 598.0 %all-gather.9.cloned.1.call-start = ((), (), s32[]{:S(2)}) async-start(), calls=%async_computation.4 | async-start | bytes 3538944 | tf_op jit(solution)/shard_map/all_gather | solution.py:56
  22.2 707.1 %reduce-scatter.4.cloned.1.call-start = ((), (), s32[]{:S(2)}) async-start(), calls=%async_computation.6 | async-start | bytes 6684672
  164.3 4.6 copy-start
  168.9 1.8 copy-start.3
  361.7 0.7 copy-start.4
  361.7 0.7 copy-start.5
  638.4 92.1 %copy-start.1 = (bf16[512,384]{1,0:T(8,128)(2,1)S(1)}, bf16[512,384]{1,0:T(8,128)(2,1)}, u32[]{:S(2)}) copy-start(bf16[512,384]{1,0:T(8,128)(2,1)} %param.8) | copy-start | bytes 1179652
Sparse Core Ops, SparseCore 0:
  9.6 154.6 all-gather.4
  165.9 186.1 all-gather.6
  353.8 191.0 all-gather.10
  546.4 73.1 all-gather.8
  638.5 90.7 reduce-scatter.3
